TPU v7x, 32 devices: a whole 2x2x4 slice. The times are simulated.
32 devices in a mesh: row: 8 (over z, x), col: 4 (over y, core).
Axes of the slice: x: 2, y: 2, z: 4, core: 2. Of those that a mesh axis runs over, the one named last changes fastest.
Arguments:
- feat: bfloat16 [256, 128, 256], P('row', 'col'), may hold values from -6 to 6
- noise_fine: float32 [256, 128, 256], P('row', 'col'), may hold values from -0.5 to 0.5
- noise_coarse: float32 [128, 64, 256], P('row', 'col'), may hold values from -0.5 to 0.5
- w_post: bfloat16 [2304, 256], replicated, may hold values from -0.125 to 0.125
- w_coarse: bfloat16 [2304, 256], replicated, may hold values from -0.125 to 0.125
- w_prior: bfloat16 [2304, 512], replicated, may hold values from -0.125 to 0.125
Outputs:
- grad_feat: bfloat16 [256, 128, 256], P('row', 'col')
- grad_post: float32 [589824], P(('row', 'col'))
- grad_coarse: float32 [589824], P(('row', 'col'))
- grad_prior: float32 [1179648], P(('row', 'col'))
All inputs are finite; a program needn't handle non-finite values.
Results may differ from a plain program's by a relative error of at most 0.0075.
Values may be sent and summed in bfloat16 or wider, within the bound.
A program may use at most 128 MiB of HBM per device.

v0:
```python
import functools
import math

import jax
import jax.numpy as jnp
from jax import lax
from jax.experimental import pallas as pl
from jax.experimental.pallas import tpu as pltpu
from jax.sharding import PartitionSpec as P

F32 = jnp.float32
BF16 = jnp.bfloat16
EDGE = 8


LANES = 128


def put(ref, at, values):
    for d in range(ref.shape[0]):
        ref[d, at, :] = values[:, d * LANES : (d + 1) * LANES]


def get(ref, at):
    return jnp.concatenate([ref[d, at, :] for d in range(ref.shape[0])], axis=1)


def tile_kernel(
    dims,
    feat,
    noise_fine,
    noise_coarse,
    w_post,
    w_coarse,
    w_prior,
    grad_feat,
    out_post,
    out_coarse,
    out_prior,
    fine,
    err,
    coarse,
    mix,
    s_feat,
    s_pool,
    s_dpr,
    x_feat,
    x_pool,
    x_ctx,
    x_dpr,
    x_gco,
    x_gfi,
    edge_fine,
    edge_coarse,
    edge_dpr,
    sums,
    outgoing,
    incoming,
    sems,
    chain_sems,
):
    s_ctx = s_gfi = s_feat
    s_gco = s_pool
    rows, cols, chans, scale, n_row, n_col = dims
    half_rows, half_cols = rows // 2, cols // 2
    r = lax.axis_index("row")
    c = lax.axis_index("col")
    has_up, has_down = r > 0, r < n_row - 1
    has_left, has_right = c > 0, c < n_col - 1
    sides = (
        (has_up, {"row": r - 1}),
        (has_down, {"row": r + 1}),
        (has_left, {"col": c - 1}),
        (has_right, {"col": c + 1}),
    )
    edge_fine[...] = jnp.zeros_like(edge_fine)
    edge_coarse[...] = jnp.zeros_like(edge_coarse)
    edge_dpr[...] = jnp.zeros_like(edge_dpr)
    for x, width, height in (
        (x_feat, cols, rows),
        (x_pool, half_cols, half_rows),
        (x_ctx, cols, rows),
        (x_dpr, cols, rows),
        (x_gco, half_cols, half_rows),
        (x_gfi, cols, rows),
    ):
        x[0:width, :] = jnp.zeros((width, x.shape[1]), x.dtype)
        x[(height + 1) * width :, :] = jnp.zeros((width, x.shape[1]), x.dtype)

    barrier = pltpu.get_barrier_semaphore()
    for has, device in sides:
        @pl.when(has)
        def _(device=device):
            pl.semaphore_signal(
                barrier, inc=1, device_id=device, device_id_type=pl.DeviceIdType.MESH
            )
    count = n_row * n_col
    bits = count.bit_length() - 1
    col_bits = n_col.bit_length() - 1
    me = r * n_col + c

    def bit_of(b):
        return me // 2**b % 2

    def partner(b):
        if b < col_bits:
            return {"col": c + 2**b * (1 - 2 * bit_of(b))}
        return {"row": r + 2 ** (b - col_bits) * (1 - 2 * bit_of(b))}

    for b in range(bits):
        pl.semaphore_signal(
            barrier, inc=1, device_id=partner(b), device_id_type=pl.DeviceIdType.MESH
        )
    pl.semaphore_wait(barrier, bits + sum(has.astype(jnp.int32) for has, _device in sides))

    def each(n, body):
        if n <= 16:
            for j in range(n):
                body(j)
        else:
            pl.loop(0, n)(body)

    def chain(number, order, out, out_at):
        acc, send, recv = sums[number], outgoing[number], incoming[number]
        state = {"step": 0, "copy": None}

        def offset(k):
            return count - (count >> k)

        def step():
            k = state["step"]
            if k > bits:
                return
            state["step"] = k + 1
            if k > 0:
                state["copy"].wait()
            if k == bits:
                out[:, out_at] = acc[me] + recv[offset(k - 1)].astype(F32)
                return
            bit = order[k]
            free = [b for b in range(bits) if b not in order[:k]]
            rest = [b for b in free if b != bit]
            place = free.index(bit)
            fixed = sum((bit_of(b) * 2**b for b in order[:k]), 0)
            n = count >> (k + 1)

            def value(j, choice):
                index = fixed + choice * 2**bit
                for q, b in enumerate(rest):
                    index = index + j // 2**q % 2 * 2**b
                total = acc[index]
                if k > 0:
                    slot = j // 2**place * 2 ** (place + 1) + choice * 2**place + j % 2**place
                    total = total + recv[offset(k - 1) + slot].astype(F32)
                return index, total

            def fill(j):
                send[offset(k) + j] = value(j, 1 - bit_of(bit))[1].astype(BF16)

            each(n, fill)
            state["copy"] = pltpu.make_async_remote_copy(
                src_ref=send.at[pl.ds(offset(k), n)],
                dst_ref=recv.at[pl.ds(offset(k), n)],
                send_sem=chain_sems.at[number, k, 0],
                recv_sem=chain_sems.at[number, k, 1],
                device_id=partner(bit),
                device_id_type=pl.DeviceIdType.MESH,
            )
            state["copy"].start()

            def keep(j):
                index, total = value(j, bit_of(bit))
                acc[index] = total

            if k > 0:
                each(n, keep)

        return step

    near, rest = [0], list(range(1, bits))
    first = near + rest
    second = near + rest[1::-1] + rest[2:]
    third = near + rest[2:3] + rest[:2] + rest[3:]
    half = chans // 2
    post_1 = chain(0, first, out_post, slice(0, half))
    post_2 = chain(1, second, out_post, slice(half, chans))
    middle = chain(2, third, out_coarse, slice(0, chans))
    prior_1 = chain(3, first, out_prior, slice(0, chans))
    prior_2 = chain(4, second, out_prior, slice(chans, 2 * chans))
    parts_post = ((sums[0], 0), (sums[1], half))
    parts_coarse = ((sums[2], 0),)
    parts_prior = ((sums[3], 0), (sums[4], chans))

    def spread(parts, start, values):
        height = values.shape[0]
        for acc, at in parts:
            per, width = acc.shape[1:]
            row = start
            while row < start + height:
                inner = row % per
                size = min(per - inner, start + height - row)
                acc[row // per, inner : inner + size] = values[
                    row - start : row - start + size, at : at + width
                ]
                row += size

    def exchange(index, s, x, edges, slot, height, width, work_1=None, work_2=None):
        stride = width + 2 * EDGE
        depth = s.shape[0] * LANES

        def copy(src, dst, k, device):
            return pltpu.make_async_remote_copy(
                src_ref=src,
                dst_ref=dst,
                send_sem=sems.at[index, k],
                recv_sem=sems.at[index, 4 + k],
                device_id=device,
                device_id_type=pl.DeviceIdType.MESH,
            )

        edges[slot, 0] = get(s, pl.ds(EDGE, height, stride=stride)).astype(BF16)
        edges[slot, 1] = get(s, pl.ds(EDGE + width - 1, height, stride=stride)).astype(BF16)
        leftward = copy(edges.at[slot, 0], edges.at[slot, 3], 0, {"col": c - 1})
        rightward = copy(edges.at[slot, 1], edges.at[slot, 2], 1, {"col": c + 1})
        pl.when(has_left)(leftward.start)
        pl.when(has_right)(rightward.start)
        for i in range(height):
            x[pl.ds((i + 1) * width, width), depth : 2 * depth] = get(
                s, pl.ds(i * stride + EDGE, width)
            ).astype(BF16)
        if work_1 is not None:
            work_1()

        @pl.when(has_left)
        def _():
            leftward.wait_send()
            rightward.wait_recv()

        @pl.when(has_right)
        def _():
            rightward.wait_send()
            leftward.wait_recv()

        put(s, pl.ds(EDGE - 1, height, stride=stride), edges[slot, 2].astype(F32))
        put(s, pl.ds(EDGE + width, height, stride=stride), edges[slot, 3].astype(F32))
        order = [0, height - 1] + list(range(1, height - 1))
        upward = copy(
            x.at[pl.ds(width, width)], x.at[pl.ds((height + 1) * width, width)], 2, {"row": r - 1}
        )
        downward = copy(
            x.at[pl.ds(height * width, width)], x.at[pl.ds(0, width)], 3, {"row": r + 1}
        )
        for n, i in enumerate(order):
            for b in (0, 2):
                x[pl.ds((i + 1) * width, width), b * depth : (b + 1) * depth] = get(
                    s, pl.ds(i * stride + EDGE - 1 + b, width)
                ).astype(BF16)
            if n == 1:
                pl.when(has_up)(upward.start)
                pl.when(has_down)(downward.start)
        if work_2 is not None:
            work_2()

        @pl.when(has_up)
        def _():
            upward.wait_send()
            downward.wait_recv()

        @pl.when(has_down)
        def _():
            downward.wait_send()
            upward.wait_recv()

    def conv(x, w, start, size, width):
        k = w.shape[0] // 3
        total = None
        for a in range(3):
            part = jnp.dot(
                x[pl.ds(start + a * width, size), :],
                w[a * k : (a + 1) * k, :],
                preferred_element_type=F32,
            )
            total = part if total is None else total + part
        return total

    def conv_back(x, w, start, size, width):
        k = w.shape[0] // 9
        depth = w.shape[1]
        total = None
        for a in range(3):
            for b in range(3):
                tap = 3 * (2 - a) + (2 - b)
                part = lax.dot_general(
                    x[pl.ds(start + a * width, size), b * depth : (b + 1) * depth],
                    w[tap * k : (tap + 1) * k, :],
                    (((1,), (1,)), ((), ())),
                    preferred_element_type=F32,
                )
                total = part if total is None else total + part
        return total

    def weight_grad(x, g, parts, height, width, taps):
        depth = x.shape[1] // 3
        g_depth = g.shape[1] // 3
        size = height * width
        own = g[pl.ds(width, size), g_depth : 2 * g_depth]
        for a in taps:
            for b in range(3):
                tap = 3 * a + b
                values = scale * lax.dot_general(
                    x[pl.ds(a * width, size), b * depth : (b + 1) * depth],
                    own,
                    (((0,), (0,)), ((), ())),
                    preferred_element_type=F32,
                )
                spread(parts, tap * depth, values)

    lines = 8
    block = lines * cols
    half_block = block // 4

    def pool_sum(values):
        paired = values.reshape(lines // 2, 2, cols, chans)
        put(mix, pl.ds(0, block // 2), (paired[:, 0] + paired[:, 1]).reshape(block // 2, chans))
        return get(mix, pl.ds(0, half_block, stride=2)) + get(mix, pl.ds(1, half_block, stride=2))

    def repeat_columns(values):
        put(mix, pl.ds(0, half_rows * half_cols, stride=2), values)
        put(mix, pl.ds(1, half_rows * half_cols, stride=2), values)

    fine_stride = cols + 2 * EDGE
    half_stride = half_cols + 2 * EDGE

    for i in range(rows):
        put(s_feat, pl.ds(i * fine_stride + EDGE, cols), feat[pl.ds(i * cols, cols), :].astype(F32))
    exchange(0, s_feat, x_feat, edge_fine, 0, rows, cols)

    for m in range(rows // lines):
        values = conv(x_feat, w_post, m * block, block, cols) + noise_fine[pl.ds(m * block, block), :]
        fine[pl.ds(m * block, block), :] = values
        pooled = (0.25 * pool_sum(values)).astype(BF16).astype(F32)
        for i in range(lines // 2):
            at = pl.ds((m * lines // 2 + i) * half_stride + EDGE, half_cols)
            put(s_pool, at, pooled[i * half_cols : (i + 1) * half_cols])
    exchange(1, s_pool, x_pool, edge_coarse, 0, half_rows, half_cols)

    values = conv(x_pool, w_coarse, 0, half_rows * half_cols, half_cols) + noise_coarse[...]
    coarse[...] = values
    repeat_columns(values.astype(BF16).astype(F32))
    for i in range(rows):
        put(s_ctx, pl.ds(i * fine_stride + EDGE, cols), get(mix, pl.ds(i // 2 * cols, cols)))
    exchange(2, s_ctx, x_ctx, edge_fine, 1, rows, cols)

    for m in range(rows // lines):
        prior = conv(x_ctx, w_prior, m * block, block, cols)
        raw = prior[:, chans:]
        small = jnp.exp(-jnp.abs(raw))
        sigma = jnp.maximum(raw, 0.0) + jnp.log1p(small) + 0.5
        gate = jnp.where(raw >= 0, 1.0, small) / (1.0 + small)
        inverse = 1.0 / sigma
        deviation = fine[pl.ds(m * block, block), :] - prior[:, :chans]
        ratio = deviation * inverse
        residual = ratio * inverse
        err[pl.ds(m * block, block), :] = residual
        slope = (inverse - ratio * ratio * inverse) * gate
        for i in range(lines):
            at = pl.ds((m * lines + i) * fine_stride + EDGE, cols)
            here = slice(i * cols, (i + 1) * cols)
            both = jnp.concatenate([-residual[here], slope[here]], axis=1)
            put(s_dpr, at, both.astype(BF16).astype(F32))
    exchange(
        3,
        s_dpr,
        x_dpr,
        edge_dpr,
        0,
        rows,
        cols,
        lambda: weight_grad(x_ctx, x_dpr, parts_prior, rows, cols, (0, 1)),
        lambda: weight_grad(x_ctx, x_dpr, parts_prior, rows, cols, (2,)),
    )

    prior_1()
    prior_2()
    for m in range(rows // lines):
        if m == 3:
            prior_1()
            prior_2()
        back = pool_sum(conv_back(x_dpr, w_prior, m * block, block, cols))
        g = (coarse[pl.ds(m * half_block, half_block), :] + back).astype(BF16).astype(F32)
        for i in range(lines // 2):
            at = pl.ds((m * lines // 2 + i) * half_stride + EDGE, half_cols)
            put(s_gco, at, g[i * half_cols : (i + 1) * half_cols])
    exchange(
        4,
        s_gco,
        x_gco,
        edge_coarse,
        1,
        half_rows,
        half_cols,
        lambda: weight_grad(x_pool, x_gco, parts_coarse, half_rows, half_cols, (0, 1)),
        lambda: weight_grad(x_pool, x_gco, parts_coarse, half_rows, half_cols, (2,)),
    )

    middle()
    repeat_columns(0.25 * conv_back(x_gco, w_coarse, 0, half_rows * half_cols, half_cols))
    for i in range(rows):
        total = err[pl.ds(i * cols, cols), :] + get(mix, pl.ds(i // 2 * cols, cols))
        put(s_gfi, pl.ds(i * fine_stride + EDGE, cols), total.astype(BF16).astype(F32))
    prior_1()
    prior_2()
    middle()
    exchange(
        5,
        s_gfi,
        x_gfi,
        edge_fine,
        2,
        rows,
        cols,
        lambda: weight_grad(x_feat, x_gfi, parts_post, rows, cols, (0, 1)),
        lambda: weight_grad(x_feat, x_gfi, parts_post, rows, cols, (2,)),
    )
    post_1()
    post_2()
    prior_1()
    prior_2()
    for m in range(rows // lines):
        if m == 2:
            post_1()
            post_2()
            middle()
        grad_feat[pl.ds(m * block, block), :] = conv_back(
            x_gfi, w_post, m * block, block, cols
        ).astype(BF16)
    for _ in range(bits + 1):
        for step in (prior_1, prior_2, middle, post_1, post_2):
            step()


def on_device(sizes, feat, noise_fine, noise_coarse, w_post, w_coarse, w_prior):
    n_row, n_col = sizes
    rows, cols, chans = feat.shape
    half_rows, half_cols = rows // 2, cols // 2
    scale = 1.0 / math.sqrt(rows * n_row * cols * n_col)
    cells, half_cells = rows * cols, half_rows * half_cols
    vmem = pl.BlockSpec(memory_space=pltpu.VMEM)

    def padded(height, width, depth):
        return pltpu.VMEM((depth // LANES, height * (width + 2 * EDGE), LANES), F32)

    def columns(height, width, depth):
        return pltpu.VMEM(((height + 2) * width, 3 * depth), BF16)

    dims = (rows, cols, chans, scale, n_row, n_col)
    count = n_row * n_col
    per = w_post.shape[0] // count
    widths = (chans // 2, chans // 2, chans, chans, chans)
    grad_feat, out_post, out_coarse, out_prior = pl.pallas_call(
        functools.partial(tile_kernel, dims),
        out_shape=(
            jax.ShapeDtypeStruct((cells, chans), BF16),
            jax.ShapeDtypeStruct((per, chans), F32),
            jax.ShapeDtypeStruct((per, chans), F32),
            jax.ShapeDtypeStruct((per, 2 * chans), F32),
        ),
        in_specs=[vmem] * 6,
        out_specs=(vmem,) * 4,
        scratch_shapes=[
            pltpu.VMEM((cells, chans), F32),
            pltpu.VMEM((cells, chans), F32),
            pltpu.VMEM((half_cells, chans), F32),
            pltpu.VMEM((chans // LANES, 2 * half_cells, LANES), F32),
            padded(rows, cols, chans),
            padded(half_rows, half_cols, chans),
            padded(rows, cols, 2 * chans),
            columns(rows, cols, chans),
            columns(half_rows, half_cols, chans),
            columns(rows, cols, chans),
            columns(rows, cols, 2 * chans),
            columns(half_rows, half_cols, chans),
            columns(rows, cols, chans),
            pltpu.VMEM((3, 4, rows, chans), BF16),
            pltpu.VMEM((2, 4, half_rows, chans), BF16),
            pltpu.VMEM((1, 4, rows, 2 * chans), BF16),
            [pltpu.VMEM((count, per, width), F32) for width in widths],
            [pltpu.VMEM((count - 1, per, width), BF16) for width in widths],
            [pltpu.VMEM((count - 1, per, width), BF16) for width in widths],
            pltpu.SemaphoreType.DMA((6, 8)),
            pltpu.SemaphoreType.DMA((5, count.bit_length() - 1, 2)),
        ],
        compiler_params=pltpu.CompilerParams(
            collective_id=0, has_side_effects=True, vmem_limit_bytes=65000 * 1024
        ),
    )(
        feat.reshape(cells, chans),
        noise_fine.reshape(cells, chans),
        noise_coarse.reshape(half_cells, chans),
        w_post,
        w_coarse,
        w_prior,
    )
    return (
        grad_feat.reshape(rows, cols, chans),
        out_post.reshape(-1),
        out_coarse.reshape(-1),
        out_prior.reshape(-1),
    )


def solution(mesh):
    sizes = (mesh.shape["row"], mesh.shape["col"])
    return jax.shard_map(
        functools.partial(on_device, sizes),
        mesh=mesh,
        in_specs=(
            P("row", "col", None),
            P("row", "col", None),
            P("row", "col", None),
            P(),
            P(),
            P(),
        ),
        out_specs=(P("row", "col", None), P(("row", "col")), P(("row", "col")), P(("row", "col"))),
        check_vma=False,
    )
```

profile of v0, /device:TPU:0, one launch (start us, length us, event | category | flops | bytes accessed | tf_op | source)
XLA Modules:
  0.0 94.9 jit_solution(15084727560708257873)
XLA Ops:
  0.6 87.7 %shard_map.93 = (bf16[1024,256]{1,0:T(8,128)(2,1)}, f32[72,256]{1,0:T(8,128)}, f32[72,256]{1,0:T(8,128)}, f32[72,512]{1,0:T(8,128)}) custom-call(bf16[1024,256]{1,0:T(8,128)(2,1)} %bitcast.11, f32[1024,256]{1,0:T(8,128)} %bitcast.10, f32[256,256]{1,0:T(8,128)} %bitcast.13, bf16[2304,256]{1,0:T(8,128)(2,1)} %w_post.1, bf16[2304,256]{1,0:T(8,128)(2,1)} %w_coarse.1, ...), custom_call_target="tpu_custom_call" | custom-call | tf_op jit(solution)/shard_map/pallas_call | solution.py:460
  88.3 1.6 %copy.10 = f32[9,2,8,128]{3,1,2,0:T(2,128)} copy(f32[9,2,8,128]{3,2,1,0:T(8,128)} %bitcast.19) | data formatting | bytes 147456
  89.9 1.6 %copy.11 = f32[9,2,8,128]{3,1,2,0:T(2,128)} copy(f32[9,2,8,128]{3,2,1,0:T(8,128)} %bitcast.18) | data formatting | bytes 147456
  91.4 1.6 %copy.12 = f32[9,4,8,128]{3,1,2,0:T(4,128)} copy(f32[9,4,8,128]{3,2,1,0:T(8,128)} %bitcast.15) | data formatting | bytes 294912
  93.0 1.9 %copy.14 = bf16[32,32,256]{2,1,0:T(8,128)(2,1)} copy(bf16[32,32,256]{2,1,0:T(8,128)(2,1)} %bitcast.12) | data formatting | bytes 1048576
where the time goes:
time: 95.2 us; the launch traced here: 94.9 us
  Pallas kernels  87.7 us (92%)
  local copies, waits for them, and re-layouts  6.58 us (7%)
    pallas_call x1, Pallas kernels, on_device(): pl.pallas_call(functools.partial(tile_kernel, dims), out_shape=(jax.Shape...  87.7 us
    unnamed x4, local copies, waits for them, and re-layouts  6.58 us

commit v1 on v0

--- a/solution.py
+++ b/solution.py
@@ -135,7 +135,13 @@
             if k > 0:
                 state["copy"].wait()
             if k == bits:
-                out[:, out_at] = acc[me] + recv[offset(k - 1)].astype(F32)
+                total = acc[me] + recv[offset(k - 1)].astype(F32)
+                per = total.shape[0]
+                stride = out.shape[0] // per
+                for d in range(total.shape[1] // LANES):
+                    out[pl.ds(out_at // LANES + d, per, stride=stride), :] = total[
+                        :, d * LANES : (d + 1) * LANES
+                    ]
                 return
             bit = order[k]
             free = [b for b in range(bits) if b not in order[:k]]
@@ -182,11 +188,11 @@
     second = near + rest[1::-1] + rest[2:]
     third = near + rest[2:3] + rest[:2] + rest[3:]
     half = chans // 2
-    post_1 = chain(0, first, out_post, slice(0, half))
-    post_2 = chain(1, second, out_post, slice(half, chans))
-    middle = chain(2, third, out_coarse, slice(0, chans))
-    prior_1 = chain(3, first, out_prior, slice(0, chans))
-    prior_2 = chain(4, second, out_prior, slice(chans, 2 * chans))
+    post_1 = chain(0, first, out_post, 0)
+    post_2 = chain(1, second, out_post, half)
+    middle = chain(2, third, out_coarse, 0)
+    prior_1 = chain(3, first, out_prior, 0)
+    prior_2 = chain(4, second, out_prior, chans)
     parts_post = ((sums[0], 0), (sums[1], half))
     parts_coarse = ((sums[2], 0),)
     parts_prior = ((sums[3], 0), (sums[4], chans))
@@ -383,7 +389,7 @@
     prior_1()
     prior_2()
     for m in range(rows // lines):
-        if m == 3:
+        if m == 2:
             prior_1()
             prior_2()
         back = pool_sum(conv_back(x_dpr, w_prior, m * block, block, cols))
@@ -403,14 +409,19 @@
         lambda: weight_grad(x_pool, x_gco, parts_coarse, half_rows, half_cols, (2,)),
     )
 
+    prior_1()
+    prior_2()
     middle()
     repeat_columns(0.25 * conv_back(x_gco, w_coarse, 0, half_rows * half_cols, half_cols))
     for i in range(rows):
         total = err[pl.ds(i * cols, cols), :] + get(mix, pl.ds(i // 2 * cols, cols))
         put(s_gfi, pl.ds(i * fine_stride + EDGE, cols), total.astype(BF16).astype(F32))
-    prior_1()
-    prior_2()
-    middle()
+    def late_work():
+        prior_1()
+        prior_2()
+        middle()
+        weight_grad(x_feat, x_gfi, parts_post, rows, cols, (2,))
+
     exchange(
         5,
         s_gfi,
@@ -420,23 +431,27 @@
         rows,
         cols,
         lambda: weight_grad(x_feat, x_gfi, parts_post, rows, cols, (0, 1)),
-        lambda: weight_grad(x_feat, x_gfi, parts_post, rows, cols, (2,)),
+        late_work,
     )
     post_1()
     post_2()
-    prior_1()
-    prior_2()
     for m in range(rows // lines):
         if m == 2:
             post_1()
             post_2()
-            middle()
+            prior_1()
+            prior_2()
         grad_feat[pl.ds(m * block, block), :] = conv_back(
             x_gfi, w_post, m * block, block, cols
         ).astype(BF16)
     for _ in range(bits + 1):
         for step in (prior_1, prior_2, middle, post_1, post_2):
             step()
+
+
+def hand_out(*refs):
+    for source, target in zip(refs[:4], refs[4:]):
+        target[...] = source[...]
 
 
 def on_device(sizes, feat, noise_fine, noise_coarse, w_post, w_coarse, w_prior):
@@ -461,9 +476,9 @@
         functools.partial(tile_kernel, dims),
         out_shape=(
             jax.ShapeDtypeStruct((cells, chans), BF16),
-            jax.ShapeDtypeStruct((per, chans), F32),
-            jax.ShapeDtypeStruct((per, chans), F32),
-            jax.ShapeDtypeStruct((per, 2 * chans), F32),
+            jax.ShapeDtypeStruct((per * chans // LANES, LANES), F32),
+            jax.ShapeDtypeStruct((per * chans // LANES, LANES), F32),
+            jax.ShapeDtypeStruct((per * 2 * chans // LANES, LANES), F32),
         ),
         in_specs=[vmem] * 6,
         out_specs=(vmem,) * 4,
@@ -501,6 +516,13 @@
         w_coarse,
         w_prior,
     )
+    results = (grad_feat, out_post, out_coarse, out_prior)
+    grad_feat, out_post, out_coarse, out_prior = pl.pallas_call(
+        hand_out,
+        out_shape=tuple(jax.ShapeDtypeStruct(a.shape, a.dtype) for a in results),
+        in_specs=[vmem] * 4,
+        out_specs=(vmem,) * 4,
+    )(*results)
     return (
         grad_feat.reshape(rows, cols, chans),
         out_post.reshape(-1),

time: 95.2 us -> 85.4 us (0.90)
  local copies, waits for them, and re-layouts: 6.58 us -> 0 us
  Pallas kernels: 87.7 us -> 84.6 us
    unnamed x4 -> x0, local copies, waits for them, and re-layouts: 6.58 us -> none
    pallas_call x1, Pallas kernels: 87.7 us -> 82.6 us  [on_device(): pl.pallas_call(functools.partial(tile_kernel, dims), out_shape=(jax.Shape...]
    pallas_call x0 -> x1, Pallas kernels: none -> 2.03 us  [on_device(): pl.pallas_call(hand_out, out_shape=tuple((jax.ShapeDtypeStruct(a.shape, a...]
where the time goes in v1:
time: 85.4 us; the launch traced here: 85.3 us
  Pallas kernels  84.6 us (99%)
    pallas_call x1, Pallas kernels, on_device(): pl.pallas_call(functools.partial(tile_kernel, dims), out_shape=(jax.Shape...  82.6 us
    pallas_call x1, Pallas kernels, on_device(): pl.pallas_call(hand_out, out_shape=tuple((jax.ShapeDtypeStruct(a.shape, a...  2.03 us

profile of v1, /device:TPU:0, one launch (start us, length us, event | category | flops | bytes accessed | tf_op | source)
XLA Modules:
  0.0 85.3 jit_solution(15514837185758705088)
XLA Ops:
  0.6 82.6 %shard_map.93 = (bf16[1024,256]{1,0:T(8,128)(2,1)}, f32[144,128]{1,0:T(8,128)}, f32[144,128]{1,0:T(8,128)}, f32[288,128]{1,0:T(8,128)}) custom-call(bf16[1024,256]{1,0:T(8,128)(2,1)} %bitcast.8, f32[1024,256]{1,0:T(8,128)} %bitcast.7, f32[256,256]{1,0:T(8,128)} %bitcast.9, bf16[2304,256]{1,0:T(8,128)(2,1)} %w_post.1, bf16[2304,256]{1,0:T(8,128)(2,1)} %w_coarse.1, ...), custom_call_target="tpu_custom_call" | custom-call | tf_op jit(solution)/shard_map/pallas_call | solution.py:475
  83.2 2.0 %shard_map.94 = (bf16[1024,256]{1,0:T(8,128)(2,1)}, f32[144,128]{1,0:T(8,128)}, f32[144,128]{1,0:T(8,128)}, f32[288,128]{1,0:T(8,128)}) custom-call(bf16[1024,256]{1,0:T(8,128)(2,1)} %get-tuple-element.12.refs_0_, f32[144,128]{1,0:T(8,128)} %get-tuple-element.13.refs_1_, f32[144,128]{1,0:T(8,128)} %get-tuple-element.14.refs_2_, ...), custom_call_target="tpu_custom_call" | custom-call | tf_op jit(solution)/shard_map/pallas_call | solution.py:520
